TPU v7x, 32 devices: a whole 2x2x4 slice. The times are simulated.
32 devices in a mesh: seq: 8 (over y, x, core), clip: 4 (over z).
Axes of the slice: x: 2, y: 2, z: 4, core: 2. Of those that a mesh axis runs over, the one named last changes fastest.
Arguments:
- queries: bfloat16 [4, 4096, 512], P('clip', 'seq'), may hold values from -8 to 8
- keys: bfloat16 [4, 4096, 512], P('clip', 'seq'), may hold values from -8 to 8
- values: bfloat16 [4, 4096, 512], P('clip', 'seq'), may hold values from -6 to 6
- out_cotangent: bfloat16 [4, 4096, 1024], P('clip', 'seq'), may hold values from -6 to 6
- visible_counts: int32 [4, 8], P('clip'), may hold values from 1 to 96, 384 in all within a row
- span_offset: int32 [4, 8], P('clip'), may hold values from 0 to 511
- out_weight: bfloat16 [512, 1024], P('seq'), may hold values from -0.1875 to 0.1875
Outputs:
- query_grads: bfloat16 [4, 4096, 512], P('clip', 'seq')
- key_grads: bfloat16 [4, 4096, 512], P('clip', 'seq')
- value_grads: bfloat16 [4, 4096, 512], P('clip', 'seq')
- weight_grad: float32 [512, 1024], P('seq')
Inputs may be any that keep to these rules, and one draw needn't show every extreme that they name: `visible_counts`: in each clip the 8 counts sum to 384, and the largest is exactly 96.
All inputs are finite; a program needn't handle non-finite values.
Results may differ from a plain program's by a relative error of at most 0.014.
Values may be sent and summed in bfloat16 or wider, within the bound.
No kernel may reach another device: no remote copies, remote signals or barrier semaphores. Data moves between devices by JAX's collectives and lax.ppermute only.
A program may use at most 64 MiB of HBM per device.

v0:
```python
import jax
import jax.numpy as jnp
from jax import lax
from jax.sharding import PartitionSpec as P

HEADS = 8
HD = 64
VIS_DEV = 48
MAXV = 96


def pick_entry(table, position):
    order = jnp.arange(table.shape[0], dtype=jnp.int32)
    chosen = jnp.where(order[None, :] == position[:, None], table[None, :], 0)
    return jnp.sum(chosen, axis=1)


def split_heads(block):
    return block.reshape(block.shape[0], HEADS, HD).transpose(1, 0, 2)


def join_heads(block):
    return block.transpose(1, 0, 2).reshape(block.shape[1], HEADS * HD)


def query_side(parts):
    query_head, key_head, value_head, dout_head = parts
    factor = HD ** (-0.5)
    scores = (
        lax.dot_general(
            query_head, key_head, (((1,), (1,)), ((), ())), preferred_element_type=jnp.float32
        )
        * factor
    )
    peak_score = jnp.max(scores, axis=1, keepdims=True)
    log_total = peak_score + jnp.log(jnp.sum(jnp.exp(scores - peak_score), axis=1, keepdims=True))
    weights = jnp.exp(scores - log_total)
    weights_low = weights.astype(jnp.bfloat16)
    attended = jnp.dot(weights_low, value_head, preferred_element_type=jnp.float32).astype(
        jnp.bfloat16
    )
    inner_sum = jnp.sum(
        dout_head.astype(jnp.float32) * attended.astype(jnp.float32), axis=1, keepdims=True
    )
    dweights = lax.dot_general(
        dout_head, value_head, (((1,), (1,)), ((), ())), preferred_element_type=jnp.float32
    )
    dscores = (weights * (dweights - inner_sum)).astype(jnp.bfloat16)
    grad_query = (jnp.dot(dscores, key_head, preferred_element_type=jnp.float32) * factor).astype(
        jnp.bfloat16
    )
    return (attended, grad_query, log_total[:, 0], inner_sum[:, 0])


def key_side_add(query_piece, dout_piece, log_piece, inner_piece, key_heads, value_heads):
    factor = HD ** (-0.5)

    def one_head(parts):
        query_head, dout_head, log_head, inner_head, key_head, value_head = parts
        scores = (
            lax.dot_general(
                query_head, key_head, (((1,), (1,)), ((), ())), preferred_element_type=jnp.float32
            )
            * factor
        )
        weights = jnp.exp(scores - log_head[:, None])
        weights_low = weights.astype(jnp.bfloat16)
        value_part = lax.dot_general(
            weights_low, dout_head, (((0,), (0,)), ((), ())), preferred_element_type=jnp.float32
        )
        dweights = lax.dot_general(
            dout_head, value_head, (((1,), (1,)), ((), ())), preferred_element_type=jnp.float32
        )
        dscores = (weights * (dweights - inner_head[:, None])).astype(jnp.bfloat16)
        key_part = lax.dot_general(
            dscores, query_head, (((0,), (0,)), ((), ())), preferred_element_type=jnp.float32
        )
        return (key_part, value_part)

    key_parts, value_parts = lax.map(
        one_head,
        (
            split_heads(query_piece),
            split_heads(dout_piece),
            log_piece.T,
            inner_piece.T,
            key_heads,
            value_heads,
        ),
    )
    return (key_parts, value_parts)


def local(queries, keys, values, out_cotangent, visible_counts, span_offset, out_weight):
    devices = lax.axis_size("seq")
    device = lax.axis_index("seq")
    frames = queries.shape[1]
    visible_rows = VIS_DEV
    capacity = MAXV // devices
    counts = visible_counts[0]
    offsets = span_offset[0]
    shard_ends = jnp.cumsum(counts)
    starts = shard_ends - counts
    this_device = device.reshape(1)
    count_here = pick_entry(counts, this_device)[0]
    start_here = pick_entry(starts, this_device)[0]
    span_begin = pick_entry(offsets, this_device)[0] % (count_here + 1)
    masked = frames - count_here
    send_slots = jnp.arange(devices * capacity, dtype=jnp.int32)
    peer_index = send_slots // capacity
    within = send_slots % capacity
    first_slot = (start_here - peer_index + devices - 1) // devices
    global_index = (first_slot + within) * devices + peer_index
    ranked = global_index - start_here
    live_slot = ranked < count_here
    frame_of = jnp.clip(jnp.where(ranked < span_begin, ranked, ranked + masked), 0, frames - 1)

    def outgoing(block):
        return jnp.where(
            live_slot[:, None], jnp.take(block[0], frame_of, axis=0), jnp.zeros((), block.dtype)
        )

    arrived = (
        lax.all_to_all(outgoing(queries), "seq", split_axis=0, concat_axis=0, tiled=True),
        lax.all_to_all(outgoing(keys), "seq", split_axis=0, concat_axis=0, tiled=True),
        lax.all_to_all(outgoing(values), "seq", split_axis=0, concat_axis=0, tiled=True),
        lax.all_to_all(outgoing(out_cotangent), "seq", split_axis=0, concat_axis=0, tiled=True),
    )
    packed_slot = jnp.arange(visible_rows, dtype=jnp.int32)
    packed_index = packed_slot * devices + device
    owner_shard = jnp.sum((shard_ends[None, :] <= packed_index[:, None]).astype(jnp.int32), axis=1)
    owner_first = (pick_entry(starts, owner_shard) - device + devices - 1) // devices
    arrived_row = owner_shard * capacity + packed_slot - owner_first
    query_pack = jnp.take(arrived[0], arrived_row, axis=0)
    key_pack = jnp.take(arrived[1], arrived_row, axis=0)
    value_pack = jnp.take(arrived[2], arrived_row, axis=0)
    cotangent_pack = jnp.take(arrived[3], arrived_row, axis=0)
    output_grad = lax.dot_general(
        cotangent_pack,
        lax.all_gather(out_weight, "seq", axis=0, tiled=True),
        (((1,), (1,)), ((), ())),
        preferred_element_type=jnp.float32,
    ).astype(jnp.bfloat16)
    key_all, value_all = (
        lax.all_gather(key_pack, "seq", axis=0, tiled=True),
        lax.all_gather(value_pack, "seq", axis=0, tiled=True),
    )
    attended, query_grad, log_totals, inner_sums = lax.map(
        query_side,
        (
            split_heads(query_pack),
            split_heads(key_all),
            split_heads(value_all),
            split_heads(output_grad),
        ),
    )
    attended = join_heads(attended)
    query_grad = join_heads(query_grad)
    log_rows = log_totals.T
    inner_rows = inner_sums.T
    partial_term = lax.dot_general(
        attended, cotangent_pack, (((0,), (0,)), ((), ())), preferred_element_type=jnp.float32
    )
    seq_sum = lax.psum_scatter(
        partial_term.astype(jnp.bfloat16), "seq", scatter_dimension=0, tiled=True
    )
    clip_sum = lax.psum(seq_sum, "clip").astype(jnp.float32)
    weight_grad = clip_sum * (lax.axis_size("clip") * visible_rows * devices) ** (-0.5)
    log_every, inner_every = (
        lax.all_gather(log_rows, "seq", axis=0, tiled=True),
        lax.all_gather(inner_rows, "seq", axis=0, tiled=True),
    )
    key_heads = split_heads(key_pack)
    value_heads = split_heads(value_pack)
    key_sum, value_sum = key_side_add(
        lax.all_gather(query_pack, "seq", axis=0, tiled=True),
        lax.all_gather(output_grad, "seq", axis=0, tiled=True),
        log_every,
        inner_every,
        key_heads,
        value_heads,
    )
    key_grad = join_heads((key_sum * HD ** (-0.5)).astype(jnp.bfloat16))
    value_grad = join_heads(value_sum.astype(jnp.bfloat16))
    back_first = (pick_entry(starts, peer_index) - device + devices - 1) // devices
    back_slot = back_first + within
    back_live = back_slot * devices + device < pick_entry(shard_ends, peer_index)
    back_row = jnp.clip(back_slot, 0, visible_rows - 1)

    def returning(block):
        return jnp.where(
            back_live[:, None], jnp.take(block, back_row, axis=0), jnp.zeros((), block.dtype)
        )

    returned = (
        lax.all_to_all(returning(query_grad), "seq", split_axis=0, concat_axis=0, tiled=True),
        lax.all_to_all(returning(key_grad), "seq", split_axis=0, concat_axis=0, tiled=True),
        lax.all_to_all(returning(value_grad), "seq", split_axis=0, concat_axis=0, tiled=True),
    )
    position = jnp.arange(frames, dtype=jnp.int32)
    visible = (position < span_begin) | (position >= span_begin + masked)
    frame_rank = jnp.where(position < span_begin, position, position - masked)
    frame_global = start_here + frame_rank
    frame_peer = frame_global % devices
    frame_slot = frame_global // devices
    frame_first = (start_here - frame_peer + devices - 1) // devices
    frame_row = jnp.clip(
        frame_peer * capacity + frame_slot - frame_first, 0, devices * capacity - 1
    )

    def placed(block):
        return jnp.where(
            visible[:, None], jnp.take(block, frame_row, axis=0), jnp.zeros((), block.dtype)
        )[None]

    return (placed(returned[0]), placed(returned[1]), placed(returned[2]), weight_grad)


def solution(mesh):
    placed = (
        P("clip", "seq", None),
        P("clip", "seq", None),
        P("clip", "seq", None),
        P("clip", "seq", None),
        P("clip", None),
        P("clip", None),
        P("seq", None),
    )
    return jax.shard_map(
        local,
        mesh=mesh,
        in_specs=placed,
        out_specs=(
            P("clip", "seq", None),
            P("clip", "seq", None),
            P("clip", "seq", None),
            P("seq", None),
        ),
        check_vma=False,
    )
```

profile of v0, /device:TPU:0, one launch (start us, length us, event | category | flops | bytes accessed | tf_op | source)
XLA Modules:
  0.0 217.8 jit_solution(15005196300830094414)
XLA Ops:
  13.5 1.9 gather_fusion.2
  17.8 5.2 %all-to-all-start = ((bf16[8,12,512]{2,1,0:T(8,128)(2,1)}), bf16[8,12,512]{2,1,0:T(8,128)(2,1)S(1)}, u32[]{:S(2)}, u32[]{:S(2)}) async-start(bf16[8,12,512]{2,1,0:T(8,128)(2,1)} %all_to_all.54), calls=%async_computation | async-start | bytes 262144 | tf_op jit(solution)/shard_map/all_to_all | solution.py:124
  29.8 4.2 %all-to-all-start.1 = ((bf16[8,12,512]{2,1,0:T(8,128)(2,1)}), bf16[8,12,512]{2,1,0:T(8,128)(2,1)S(1)}, u32[]{:S(2)}, u32[]{:S(2)}) async-start(bf16[8,12,512]{2,1,0:T(8,128)(2,1)} %all_to_all.57), calls=%async_computation.1 | async-start | bytes 262144 | tf_op jit(solution)/shard_map/all_to_all | solution.py:125
  34.0 6.9 %all-to-all-done.1 = bf16[8,12,512]{2,1,0:T(8,128)(2,1)S(1)} async-done(((bf16[8,12,512]{2,1,0:T(8,128)(2,1)}), bf16[8,12,512]{2,1,0:T(8,128)(2,1)S(1)}, u32[]{:S(2)}, u32[]{:S(2)}) %all-to-all-start.1) | async-done | bytes 98336 | tf_op jit(solution)/shard_map/all_to_all | solution.py:125
  40.9 3.4 %all-to-all-start.2 = ((bf16[8,12,512]{2,1,0:T(8,128)(2,1)}), bf16[8,12,512]{2,1,0:T(8,128)(2,1)S(1)}, u32[]{:S(2)}, u32[]{:S(2)}) async-start(bf16[8,12,512]{2,1,0:T(8,128)(2,1)} %all_to_all.60), calls=%async_computation.2 | async-start | bytes 262144 | tf_op jit(solution)/shard_map/all_to_all | solution.py:126
  46.3 4.7 %all-to-all-done.2 = bf16[8,12,512]{2,1,0:T(8,128)(2,1)S(1)} async-done(((bf16[8,12,512]{2,1,0:T(8,128)(2,1)}), bf16[8,12,512]{2,1,0:T(8,128)(2,1)S(1)}, u32[]{:S(2)}, u32[]{:S(2)}) %all-to-all-start.2) | async-done | bytes 98336 | tf_op jit(solution)/shard_map/all_to_all | solution.py:126
  51.1 3.4 %all-to-all-start.3 = ((bf16[8,12,1024]{2,1,0:T(8,128)(2,1)}), bf16[8,12,1024]{2,1,0:T(8,128)(2,1)S(1)}, u32[]{:S(2)}, u32[]{:S(2)}) async-start(bf16[8,12,1024]{2,1,0:T(8,128)(2,1)} %select_select_fusion.3), calls=%async_computation.3 | async-start | bytes 524288 | tf_op jit(solution)/shard_map/all_to_all | solution.py:127
  55.4 10.0 %all_gather.21 = bf16[384,512]{1,0:T(8,128)(2,1)S(1)} all-gather(bf16[48,512]{1,0:T(8,128)(2,1)S(1)} %get-tuple-element.249), channel_id=1, replica_groups=mesh['seq'=8,'clip'=4] {'seq'}, dimensions={0}, use_global_device_ids=true | all-gather | bytes 442368 | tf_op jit(solution)/shard_map/all_gather | solution.py:145
  65.7 9.5 %all_gather.22 = bf16[384,512]{1,0:T(8,128)(2,1)S(1)} all-gather(bf16[48,512]{1,0:T(8,128)(2,1)S(1)} %get-tuple-element.248), channel_id=1, replica_groups=mesh['seq'=8,'clip'=4] {'seq'}, dimensions={0}, use_global_device_ids=true | all-gather | bytes 442368 | tf_op jit(solution)/shard_map/all_gather | solution.py:146
  75.6 8.6 %all_gather.24 = bf16[384,512]{1,0:T(8,128)(2,1)S(1)} all-gather(bf16[48,512]{1,0:T(8,128)(2,1)S(1)} %get-tuple-element.250), channel_id=1, replica_groups=mesh['seq'=8,'clip'=4] {'seq'}, dimensions={0}, use_global_device_ids=true | all-gather | bytes 442368 | tf_op jit(solution)/shard_map/all_gather | solution.py:176
  87.1 9.5 %all_gather.26 = bf16[384,512]{1,0:T(8,128)(2,1)S(1)} all-gather(bf16[48,512]{1,0:T(8,128)(2,1)S(1)} %convolution_convert_fusion.2), channel_id=1, replica_groups=mesh['seq'=8,'clip'=4] {'seq'}, dimensions={0}, use_global_device_ids=true | all-gather | bytes 442368 | tf_op jit(solution)/shard_map/all_gather | solution.py:177
  96.6 18.4 %while.28 = (s32[]{:T(128)}, bf16[8,48,64]{2,1,0:T(8,128)(2,1)}, bf16[8,48,64]{2,1,0:T(8,128)(2,1)}, f32[8,48]{1,0:T(8,128)S(1)}, f32[8,48]{1,0:T(8,128)S(1)}, /...) while((s32[]{:T(128)}, bf16[8,48,64]{2,1,0:T(8,128)(2,1)}, ...), condition=%wide.region_12.15_spmd, body=%wide.region_8.14_spmd.sunk | while | flops 9642914 | bytes 566969 | solution.py:148
  115.1 8.3 %all-gather = f32[8,48,8]{1,2,0:T(8,128)S(1)} all-gather(f32[1,48,8]{1,2,0:T(8,128)S(1)} %bitcast.209), channel_id=1, replica_groups=mesh['seq'=8,'clip'=4] {'seq'}, dimensions={0}, use_global_device_ids=true | all-gather | bytes 13824 | tf_op jit(solution)/shard_map/all_gather | solution.py:170
  123.5 9.1 %all-gather.1 = f32[8,48,8]{1,2,0:T(8,128)S(1)} all-gather(f32[1,48,8]{1,2,0:T(8,128)S(1)} %bitcast.210), channel_id=1, replica_groups=mesh['seq'=8,'clip'=4] {'seq'}, dimensions={0}, use_global_device_ids=true | all-gather | bytes 13824 | tf_op jit(solution)/shard_map/all_gather | solution.py:171
  134.5 5.0 %while.29 = (s32[]{:T(128)}, f32[8,48,64]{2,1,0:T(8,128)S(1)}, bf16[8,48,64]{2,1,0:T(8,128)(2,1)S(1)}, bf16[8,384,64]{1,2,0:T(8,128)(2,1)S(1)}, bf16[8,48,64]{2,...) while((s32[]{:T(128)}, f32[8,48,64]{2,1,0:T(8,128)S(1)}, ...), condition=%wide.region_14.19_spmd, body=%wide.region_13.18_spmd.sunk | while | flops 9547778 | bytes 505961 | solution.py:80
  143.2 3.4 %all-to-all-start.4 = ((bf16[8,12,512]{2,1,0:T(8,128)(2,1)}), bf16[8,12,512]{2,1,0:T(8,128)(2,1)S(1)}, u32[]{:S(2)}, u32[]{:S(2)}) async-start(bf16[8,12,512]{2,1,0:T(8,128)(2,1)} %all_to_all.65), calls=%async_computation.4 | async-start | bytes 262144 | tf_op jit(solution)/shard_map/all_to_all | solution.py:196
  147.2 4.7 %all-to-all-done.4 = bf16[8,12,512]{2,1,0:T(8,128)(2,1)S(1)} async-done(((bf16[8,12,512]{2,1,0:T(8,128)(2,1)}), bf16[8,12,512]{2,1,0:T(8,128)(2,1)S(1)}, u32[]{:S(2)}, u32[]{:S(2)}) %all-to-all-start.4) | async-done | bytes 98336 | tf_op jit(solution)/shard_map/all_to_all | solution.py:196
  152.0 3.4 %all-to-all-start.5 = ((bf16[8,12,512]{2,1,0:T(8,128)(2,1)}), bf16[8,12,512]{2,1,0:T(8,128)(2,1)S(1)}, u32[]{:S(2)}, u32[]{:S(2)}) async-start(bf16[8,12,512]{2,1,0:T(8,128)(2,1)} %all_to_all.68), calls=%async_computation.5 | async-start | bytes 262144 | tf_op jit(solution)/shard_map/all_to_all | solution.py:197
  156.7 5.5 %all-to-all-done.5 = bf16[8,12,512]{2,1,0:T(8,128)(2,1)S(1)} async-done(((bf16[8,12,512]{2,1,0:T(8,128)(2,1)}), bf16[8,12,512]{2,1,0:T(8,128)(2,1)S(1)}, u32[]{:S(2)}, u32[]{:S(2)}) %all-to-all-start.5) | async-done | bytes 98336 | tf_op jit(solution)/shard_map/all_to_all | solution.py:197
  162.2 3.4 %all-to-all-start.6 = ((bf16[8,12,512]{2,1,0:T(8,128)(2,1)}), bf16[8,12,512]{2,1,0:T(8,128)(2,1)S(1)}, u32[]{:S(2)}, u32[]{:S(2)}) async-start(bf16[8,12,512]{2,1,0:T(8,128)(2,1)} %all_to_all.71), calls=%async_computation.6 | async-start | bytes 262144 | tf_op jit(solution)/shard_map/all_to_all | solution.py:198
  165.9 2.0 gather_fusion.9
  167.9 2.0 gather_fusion.11
  171.7 2.0 gather_fusion.13
  175.1 34.6 %all-reduce.2.cloned.1.call-done = bf16[64,1024]{1,0:T(8,128)(2,1)} async-done(((bf16[64,1024]{1,0:T(8,128)(2,1)}), bf16[64,1024]{1,0:T(8,128)(2,1)}) %all-reduce.2.cloned.1.call-update) | async-done | bytes 131088 | tf_op jit(solution)/shard_map/psum | solution.py:167
  (207 shorter events, 55.5 us)
Async XLA Ops:
  7.2 19.5 %copy-start = (bf16[1,512,1024]{2,1,0:T(8,128)(2,1)S(1)}, bf16[1,512,1024]{2,1,0:T(8,128)(2,1)}, u32[]{:S(2)}) copy-start(bf16[1,512,1024]{2,1,0:T(8,128)(2,1)} %param.22) | copy-start | bytes 3145732
  7.2 8.2 %copy-start.1 = (bf16[1,512,512]{2,1,0:T(8,128)(2,1)S(1)}, bf16[1,512,512]{2,1,0:T(8,128)(2,1)}, u32[]{:S(2)}) copy-start(bf16[1,512,512]{2,1,0:T(8,128)(2,1)} %param.20) | copy-start | bytes 1572868
  7.2 9.0 %copy-start.2 = (bf16[1,512,512]{2,1,0:T(8,128)(2,1)S(1)}, bf16[1,512,512]{2,1,0:T(8,128)(2,1)}, u32[]{:S(2)}) copy-start(bf16[1,512,512]{2,1,0:T(8,128)(2,1)} %param.21) | copy-start | bytes 1572868
  17.8 12.0 %all-to-all-start = ((bf16[8,12,512]{2,1,0:T(8,128)(2,1)}), bf16[8,12,512]{2,1,0:T(8,128)(2,1)S(1)}, u32[]{:S(2)}, u32[]{:S(2)}) async-start(bf16[8,12,512]{2,1,0:T(8,128)(2,1)} %all_to_all.54), calls=%async_computation | async-start | bytes 262144 | tf_op jit(solution)/shard_map/all_to_all | solution.py:124
  23.0 62.3 %all-gather.4.cloned.1.call-start = ((), (), s32[]{:S(2)}) async-start(), calls=%async_computation.8 | async-start | bytes 1179648 | tf_op jit(solution)/shard_map/all_gather | solution.py:140
  29.8 11.1 %all-to-all-start.1 = ((bf16[8,12,512]{2,1,0:T(8,128)(2,1)}), bf16[8,12,512]{2,1,0:T(8,128)(2,1)S(1)}, u32[]{:S(2)}, u32[]{:S(2)}) async-start(bf16[8,12,512]{2,1,0:T(8,128)(2,1)} %all_to_all.57), calls=%async_computation.1 | async-start | bytes 262144 | tf_op jit(solution)/shard_map/all_to_all | solution.py:125
  40.9 10.2 %all-to-all-start.2 = ((bf16[8,12,512]{2,1,0:T(8,128)(2,1)}), bf16[8,12,512]{2,1,0:T(8,128)(2,1)S(1)}, u32[]{:S(2)}, u32[]{:S(2)}) async-start(bf16[8,12,512]{2,1,0:T(8,128)(2,1)} %all_to_all.60), calls=%async_computation.2 | async-start | bytes 262144 | tf_op jit(solution)/shard_map/all_to_all | solution.py:126
  51.1 33.5 %all-to-all-start.3 = ((bf16[8,12,1024]{2,1,0:T(8,128)(2,1)}), bf16[8,12,1024]{2,1,0:T(8,128)(2,1)S(1)}, u32[]{:S(2)}, u32[]{:S(2)}) async-start(bf16[8,12,1024]{2,1,0:T(8,128)(2,1)} %select_select_fusion.3), calls=%async_computation.3 | async-start | bytes 524288 | tf_op jit(solution)/shard_map/all_to_all | solution.py:127
  54.5 119.2 %reduce-scatter.2.cloned.1.call-start = ((), (), s32[]{:S(2)}) async-start(), calls=%async_computation.9 | async-start | bytes 1179648 | tf_op jit(solution)/shard_map/reduce_scatter | solution.py:164
  115.1 17.8 %copy-start.4 = (bf16[8,48,64]{2,1,0:T(8,128)(2,1)S(1)}, bf16[8,48,64]{2,1,0:T(8,128)(2,1)}, u32[]{:S(2)}) copy-start(bf16[8,48,64]{2,1,0:T(8,128)(2,1)} %get-tuple-element.111) | copy-start | bytes 147460
  133.0 1.5 copy-start.3
  139.7 1.7 copy-start.5
  143.2 8.8 %all-to-all-start.4 = ((bf16[8,12,512]{2,1,0:T(8,128)(2,1)}), bf16[8,12,512]{2,1,0:T(8,128)(2,1)S(1)}, u32[]{:S(2)}, u32[]{:S(2)}) async-start(bf16[8,12,512]{2,1,0:T(8,128)(2,1)} %all_to_all.65), calls=%async_computation.4 | async-start | bytes 262144 | tf_op jit(solution)/shard_map/all_to_all | solution.py:196
  152.0 10.3 %all-to-all-start.5 = ((bf16[8,12,512]{2,1,0:T(8,128)(2,1)}), bf16[8,12,512]{2,1,0:T(8,128)(2,1)S(1)}, u32[]{:S(2)}, u32[]{:S(2)}) async-start(bf16[8,12,512]{2,1,0:T(8,128)(2,1)} %all_to_all.68), calls=%async_computation.5 | async-start | bytes 262144 | tf_op jit(solution)/shard_map/all_to_all | solution.py:197
  162.2 9.4 %all-to-all-start.6 = ((bf16[8,12,512]{2,1,0:T(8,128)(2,1)}), bf16[8,12,512]{2,1,0:T(8,128)(2,1)S(1)}, u32[]{:S(2)}, u32[]{:S(2)}) async-start(bf16[8,12,512]{2,1,0:T(8,128)(2,1)} %all_to_all.71), calls=%async_computation.6 | async-start | bytes 262144 | tf_op jit(solution)/shard_map/all_to_all | solution.py:198
  165.6 44.0 %all-reduce.2.cloned.1.call-start = ((), (), s32[]{:S(2)}) async-start(), calls=%async_computation.10 | async-start | bytes 262144 | tf_op jit(solution)/shard_map/psum | solution.py:167
Sparse Core Ops, SparseCore 0:
  25.7 27.5 all-gather.3
  134.6 38.3 reduce-scatter.1
  175.3 34.3 all-reduce.1
where the time goes:
time: 219 us; the launch traced here: 218 us
  waiting for transfers between devices  59 us (27%)
  blocking collectives  55 us (25%)
  starting transfers between devices  26.6 us (12%)
  matrix products  23 us (11%)
  local copies, waits for them, and re-layouts  22.3 us (10%)
  between operations  16.3 us (7%)
  other arithmetic  15.3 us (7%)
    psum x1, waiting for transfers between devices, local(): clip_sum = lax.psum(seq_sum, 'clip').astype(jnp.float32)  34.6 us
    all_gather x1, blocking collectives, local(): lax.all_gather(key_pack, 'seq', axis=0, tiled=True)  9.95 us
    all_gather x1, blocking collectives, local(): lax.all_gather(value_pack, 'seq', axis=0, tiled=True)  9.54 us
    all_gather x1, blocking collectives, local(): lax.all_gather(output_grad, 'seq', axis=0, tiled=True)  9.54 us
    all_gather x1, blocking collectives, local(): lax.all_gather(inner_rows, 'seq', axis=0, tiled=True)  9.06 us
    all_gather x1, blocking collectives, local(): lax.all_gather(query_pack, 'seq', axis=0, tiled=True)  8.62 us
    all_gather x1, blocking collectives, local(): lax.all_gather(log_rows, 'seq', axis=0, tiled=True)  8.29 us
    dot_general x8, matrix products, query_side(): jnp.dot(dscores, key_head, preferred_element_type=jnp.float32) * factor  6.93 us
  transfers between devices with their start and end apart: 10, of which 6 were waited for; matrix products, arithmetic and copies ran while one was open for 11% of the time, Pallas kernels for 0%

commit v1 on v0

--- a/solution.py
+++ b/solution.py
@@ -2,6 +2,7 @@
 import jax.numpy as jnp
 from jax import lax
 from jax.sharding import PartitionSpec as P
+from jax.lax import all_gather
 
 HEADS = 8
 HD = 64
@@ -164,7 +165,11 @@
     seq_sum = lax.psum_scatter(
         partial_term.astype(jnp.bfloat16), "seq", scatter_dimension=0, tiled=True
     )
-    clip_sum = lax.psum(seq_sum, "clip").astype(jnp.float32)
+
+    def _note_tokens(inner_x):
+        return jnp.sum(all_gather(inner_x, "clip"), axis=0)
+
+    clip_sum = _note_tokens(seq_sum).astype(jnp.float32)
     weight_grad = clip_sum * (lax.axis_size("clip") * visible_rows * devices) ** (-0.5)
     log_every, inner_every = (
         lax.all_gather(log_rows, "seq", axis=0, tiled=True),

time: 219 us -> 199 us (0.909)
  waiting for transfers between devices: 59 us -> 24.4 us
  blocking collectives: 55 us -> 70.1 us
    psum x1 -> x0, waiting for transfers between devices: 34.6 us -> none  [local(): clip_sum = lax.psum(seq_sum, 'clip').astype(jnp.float32)]
    all_gather x0 -> x1, blocking collectives: none -> 15.1 us  [_note_tokens(): return jnp.sum(all_gather(inner_x, 'clip'), axis=0)]
  transfers between devices with their start and end apart: 10 -> 9, of which waited for: 6 -> 5; matrix products, arithmetic and copies ran while one was open for 11% -> 12% of each run, Pallas kernels for 0% -> 0%
where the time goes in v1:
time: 199 us; the launch traced here: 198 us
  blocking collectives  70.1 us (35%)
  starting transfers between devices  26.6 us (13%)
  waiting for transfers between devices  24.4 us (12%)
  matrix products  23 us (12%)
  local copies, waits for them, and re-layouts  22.3 us (11%)
  between operations  16.5 us (8%)
  other arithmetic  14.5 us (7%)
    all_gather x1, blocking collectives, _note_tokens(): return jnp.sum(all_gather(inner_x, 'clip'), axis=0)  15.1 us
    all_gather x1, blocking collectives, local(): lax.all_gather(key_pack, 'seq', axis=0, tiled=True)  9.95 us
    all_gather x1, blocking collectives, local(): lax.all_gather(value_pack, 'seq', axis=0, tiled=True)  9.54 us
    all_gather x1, blocking collectives, local(): lax.all_gather(output_grad, 'seq', axis=0, tiled=True)  9.54 us
    all_gather x1, blocking collectives, local(): lax.all_gather(inner_rows, 'seq', axis=0, tiled=True)  9.06 us
    all_gather x1, blocking collectives, local(): lax.all_gather(query_pack, 'seq', axis=0, tiled=True)  8.62 us
    all_gather x1, blocking collectives, local(): lax.all_gather(log_rows, 'seq', axis=0, tiled=True)  8.29 us
    dot_general x8, matrix products, query_side(): jnp.dot(dscores, key_head, preferred_element_type=jnp.float32) * factor  6.93 us
  transfers between devices with their start and end apart: 9, of which 5 were waited for; matrix products, arithmetic and copies ran while one was open for 12% of the time, Pallas kernels for 0%

profile of v1, /device:TPU:0, one launch (start us, length us, event | category | flops | bytes accessed | tf_op | source)
XLA Modules:
  0.0 197.8 jit_solution(14398295590541453359)
XLA Ops:
  13.5 1.9 gather_fusion.2
  17.8 5.2 %all-to-all-start = ((bf16[8,12,512]{2,1,0:T(8,128)(2,1)}), bf16[8,12,512]{2,1,0:T(8,128)(2,1)S(1)}, u32[]{:S(2)}, u32[]{:S(2)}) async-start(bf16[8,12,512]{2,1,0:T(8,128)(2,1)} %all_to_all.54), calls=%async_computation | async-start | bytes 262144 | tf_op jit(solution)/shard_map/all_to_all | solution.py:125
  29.8 4.2 %all-to-all-start.1 = ((bf16[8,12,512]{2,1,0:T(8,128)(2,1)}), bf16[8,12,512]{2,1,0:T(8,128)(2,1)S(1)}, u32[]{:S(2)}, u32[]{:S(2)}) async-start(bf16[8,12,512]{2,1,0:T(8,128)(2,1)} %all_to_all.57), calls=%async_computation.1 | async-start | bytes 262144 | tf_op jit(solution)/shard_map/all_to_all | solution.py:126
  34.0 6.9 %all-to-all-done.1 = bf16[8,12,512]{2,1,0:T(8,128)(2,1)S(1)} async-done(((bf16[8,12,512]{2,1,0:T(8,128)(2,1)}), bf16[8,12,512]{2,1,0:T(8,128)(2,1)S(1)}, u32[]{:S(2)}, u32[]{:S(2)}) %all-to-all-start.1) | async-done | bytes 98336 | tf_op jit(solution)/shard_map/all_to_all | solution.py:126
  40.9 3.4 %all-to-all-start.2 = ((bf16[8,12,512]{2,1,0:T(8,128)(2,1)}), bf16[8,12,512]{2,1,0:T(8,128)(2,1)S(1)}, u32[]{:S(2)}, u32[]{:S(2)}) async-start(bf16[8,12,512]{2,1,0:T(8,128)(2,1)} %all_to_all.60), calls=%async_computation.2 | async-start | bytes 262144 | tf_op jit(solution)/shard_map/all_to_all | solution.py:127
  46.3 4.7 %all-to-all-done.2 = bf16[8,12,512]{2,1,0:T(8,128)(2,1)S(1)} async-done(((bf16[8,12,512]{2,1,0:T(8,128)(2,1)}), bf16[8,12,512]{2,1,0:T(8,128)(2,1)S(1)}, u32[]{:S(2)}, u32[]{:S(2)}) %all-to-all-start.2) | async-done | bytes 98336 | tf_op jit(solution)/shard_map/all_to_all | solution.py:127
  51.1 3.4 %all-to-all-start.3 = ((bf16[8,12,1024]{2,1,0:T(8,128)(2,1)}), bf16[8,12,1024]{2,1,0:T(8,128)(2,1)S(1)}, u32[]{:S(2)}, u32[]{:S(2)}) async-start(bf16[8,12,1024]{2,1,0:T(8,128)(2,1)} %select_select_fusion.3), calls=%async_computation.3 | async-start | bytes 524288 | tf_op jit(solution)/shard_map/all_to_all | solution.py:128
  55.4 10.0 %all_gather.27 = bf16[384,512]{1,0:T(8,128)(2,1)S(1)} all-gather(bf16[48,512]{1,0:T(8,128)(2,1)S(1)} %get-tuple-element.249), channel_id=1, replica_groups=mesh['seq'=8,'clip'=4] {'seq'}, dimensions={0}, use_global_device_ids=true | all-gather | bytes 442368 | tf_op jit(solution)/shard_map/all_gather | solution.py:146
  65.7 9.5 %all_gather.28 = bf16[384,512]{1,0:T(8,128)(2,1)S(1)} all-gather(bf16[48,512]{1,0:T(8,128)(2,1)S(1)} %get-tuple-element.248), channel_id=1, replica_groups=mesh['seq'=8,'clip'=4] {'seq'}, dimensions={0}, use_global_device_ids=true | all-gather | bytes 442368 | tf_op jit(solution)/shard_map/all_gather | solution.py:147
  75.6 8.6 %all_gather.30 = bf16[384,512]{1,0:T(8,128)(2,1)S(1)} all-gather(bf16[48,512]{1,0:T(8,128)(2,1)S(1)} %get-tuple-element.250), channel_id=1, replica_groups=mesh['seq'=8,'clip'=4] {'seq'}, dimensions={0}, use_global_device_ids=true | all-gather | bytes 442368 | tf_op jit(solution)/shard_map/all_gather | solution.py:181
  87.1 9.5 %all_gather.32 = bf16[384,512]{1,0:T(8,128)(2,1)S(1)} all-gather(bf16[48,512]{1,0:T(8,128)(2,1)S(1)} %convolution_convert_fusion.2), channel_id=1, replica_groups=mesh['seq'=8,'clip'=4] {'seq'}, dimensions={0}, use_global_device_ids=true | all-gather | bytes 442368 | tf_op jit(solution)/shard_map/all_gather | solution.py:182
  96.6 18.4 %while.28 = (s32[]{:T(128)}, bf16[8,48,64]{2,1,0:T(8,128)(2,1)}, bf16[8,48,64]{2,1,0:T(8,128)(2,1)}, f32[8,48]{1,0:T(8,128)S(1)}, f32[8,48]{1,0:T(8,128)S(1)}, /...) while((s32[]{:T(128)}, bf16[8,48,64]{2,1,0:T(8,128)(2,1)}, ...), condition=%wide.region_12.15_spmd, body=%wide.region_8.14_spmd.sunk | while | flops 9642914 | bytes 566969 | solution.py:149
  115.1 8.3 %all-gather.1 = f32[8,48,8]{1,2,0:T(8,128)S(1)} all-gather(f32[1,48,8]{1,2,0:T(8,128)S(1)} %bitcast.211), channel_id=1, replica_groups=mesh['seq'=8,'clip'=4] {'seq'}, dimensions={0}, use_global_device_ids=true | all-gather | bytes 13824 | tf_op jit(solution)/shard_map/all_gather | solution.py:175
  123.5 9.1 %all-gather.2 = f32[8,48,8]{1,2,0:T(8,128)S(1)} all-gather(f32[1,48,8]{1,2,0:T(8,128)S(1)} %bitcast.212), channel_id=1, replica_groups=mesh['seq'=8,'clip'=4] {'seq'}, dimensions={0}, use_global_device_ids=true | all-gather | bytes 13824 | tf_op jit(solution)/shard_map/all_gather | solution.py:176
  134.5 5.0 %while.29 = (s32[]{:T(128)}, f32[8,48,64]{2,1,0:T(8,128)S(1)}, bf16[8,48,64]{2,1,0:T(8,128)(2,1)S(1)}, bf16[8,384,64]{1,2,0:T(8,128)(2,1)S(1)}, bf16[8,48,64]{2,...) while((s32[]{:T(128)}, f32[8,48,64]{2,1,0:T(8,128)S(1)}, ...), condition=%wide.region_14.19_spmd, body=%wide.region_13.18_spmd.sunk | while | flops 9547778 | bytes 505961 | solution.py:81
  143.2 3.4 %all-to-all-start.4 = ((bf16[8,12,512]{2,1,0:T(8,128)(2,1)}), bf16[8,12,512]{2,1,0:T(8,128)(2,1)S(1)}, u32[]{:S(2)}, u32[]{:S(2)}) async-start(bf16[8,12,512]{2,1,0:T(8,128)(2,1)} %all_to_all.65), calls=%async_computation.4 | async-start | bytes 262144 | tf_op jit(solution)/shard_map/all_to_all | solution.py:201
  147.2 4.7 %all-to-all-done.4 = bf16[8,12,512]{2,1,0:T(8,128)(2,1)S(1)} async-done(((bf16[8,12,512]{2,1,0:T(8,128)(2,1)}), bf16[8,12,512]{2,1,0:T(8,128)(2,1)S(1)}, u32[]{:S(2)}, u32[]{:S(2)}) %all-to-all-start.4) | async-done | bytes 98336 | tf_op jit(solution)/shard_map/all_to_all | solution.py:201
  152.0 3.4 %all-to-all-start.5 = ((bf16[8,12,512]{2,1,0:T(8,128)(2,1)}), bf16[8,12,512]{2,1,0:T(8,128)(2,1)S(1)}, u32[]{:S(2)}, u32[]{:S(2)}) async-start(bf16[8,12,512]{2,1,0:T(8,128)(2,1)} %all_to_all.68), calls=%async_computation.5 | async-start | bytes 262144 | tf_op jit(solution)/shard_map/all_to_all | solution.py:202
  156.7 5.5 %all-to-all-done.5 = bf16[8,12,512]{2,1,0:T(8,128)(2,1)S(1)} async-done(((bf16[8,12,512]{2,1,0:T(8,128)(2,1)}), bf16[8,12,512]{2,1,0:T(8,128)(2,1)S(1)}, u32[]{:S(2)}, u32[]{:S(2)}) %all-to-all-start.5) | async-done | bytes 98336 | tf_op jit(solution)/shard_map/all_to_all | solution.py:202
  162.2 3.6 %all-to-all-start.6 = ((bf16[8,12,512]{2,1,0:T(8,128)(2,1)}), bf16[8,12,512]{2,1,0:T(8,128)(2,1)S(1)}, u32[]{:S(2)}, u32[]{:S(2)}) async-start(bf16[8,12,512]{2,1,0:T(8,128)(2,1)} %all_to_all.71), calls=%async_computation.6 | async-start | bytes 262144 | tf_op jit(solution)/shard_map/all_to_all | solution.py:203
  165.9 2.0 gather_fusion.9
  167.9 2.0 gather_fusion.11
  171.7 2.0 gather_fusion.13
  175.1 15.1 %all-gather = bf16[256,1024]{1,0:T(8,128)(2,1)S(1)} all-gather(bf16[64,1024]{1,0:T(8,128)(2,1)} %reduce-scatter.2.cloned.1.call-done), channel_id=2, replica_groups=mesh['seq'=8,'clip'=4] {'clip'}, dimensions={0}, use_global_device_ids=true | all-gather | bytes 655360 | tf_op jit(solution)/shard_map/all_gather | solution.py:170
  (206 shorter events, 54.5 us)
Async XLA Ops:
  7.2 19.5 %copy-start = (bf16[1,512,1024]{2,1,0:T(8,128)(2,1)S(1)}, bf16[1,512,1024]{2,1,0:T(8,128)(2,1)}, u32[]{:S(2)}) copy-start(bf16[1,512,1024]{2,1,0:T(8,128)(2,1)} %param.22) | copy-start | bytes 3145732
  7.2 8.2 %copy-start.1 = (bf16[1,512,512]{2,1,0:T(8,128)(2,1)S(1)}, bf16[1,512,512]{2,1,0:T(8,128)(2,1)}, u32[]{:S(2)}) copy-start(bf16[1,512,512]{2,1,0:T(8,128)(2,1)} %param.20) | copy-start | bytes 1572868
  7.2 9.0 %copy-start.2 = (bf16[1,512,512]{2,1,0:T(8,128)(2,1)S(1)}, bf16[1,512,512]{2,1,0:T(8,128)(2,1)}, u32[]{:S(2)}) copy-start(bf16[1,512,512]{2,1,0:T(8,128)(2,1)} %param.21) | copy-start | bytes 1572868
  17.8 12.0 %all-to-all-start = ((bf16[8,12,512]{2,1,0:T(8,128)(2,1)}), bf16[8,12,512]{2,1,0:T(8,128)(2,1)S(1)}, u32[]{:S(2)}, u32[]{:S(2)}) async-start(bf16[8,12,512]{2,1,0:T(8,128)(2,1)} %all_to_all.54), calls=%async_computation | async-start | bytes 262144 | tf_op jit(solution)/shard_map/all_to_all | solution.py:125
  23.0 62.3 %all-gather.5.cloned.1.call-start = ((), (), s32[]{:S(2)}) async-start(), calls=%async_computation.8 | async-start | bytes 1179648 | tf_op jit(solution)/shard_map/all_gather | solution.py:141
  29.8 11.1 %all-to-all-start.1 = ((bf16[8,12,512]{2,1,0:T(8,128)(2,1)}), bf16[8,12,512]{2,1,0:T(8,128)(2,1)S(1)}, u32[]{:S(2)}, u32[]{:S(2)}) async-start(bf16[8,12,512]{2,1,0:T(8,128)(2,1)} %all_to_all.57), calls=%async_computation.1 | async-start | bytes 262144 | tf_op jit(solution)/shard_map/all_to_all | solution.py:126
  40.9 10.2 %all-to-all-start.2 = ((bf16[8,12,512]{2,1,0:T(8,128)(2,1)}), bf16[8,12,512]{2,1,0:T(8,128)(2,1)S(1)}, u32[]{:S(2)}, u32[]{:S(2)}) async-start(bf16[8,12,512]{2,1,0:T(8,128)(2,1)} %all_to_all.60), calls=%async_computation.2 | async-start | bytes 262144 | tf_op jit(solution)/shard_map/all_to_all | solution.py:127
  51.1 33.5 %all-to-all-start.3 = ((bf16[8,12,1024]{2,1,0:T(8,128)(2,1)}), bf16[8,12,1024]{2,1,0:T(8,128)(2,1)S(1)}, u32[]{:S(2)}, u32[]{:S(2)}) async-start(bf16[8,12,1024]{2,1,0:T(8,128)(2,1)} %select_select_fusion.3), calls=%async_computation.3 | async-start | bytes 524288 | tf_op jit(solution)/shard_map/all_to_all | solution.py:128
  54.5 120.6 %reduce-scatter.2.cloned.1.call-start = ((), (), s32[]{:S(2)}) async-start(), calls=%async_computation.9 | async-start | bytes 1179648 | tf_op jit(solution)/shard_map/reduce_scatter | solution.py:165
  115.1 17.8 %copy-start.4 = (bf16[8,48,64]{2,1,0:T(8,128)(2,1)S(1)}, bf16[8,48,64]{2,1,0:T(8,128)(2,1)}, u32[]{:S(2)}) copy-start(bf16[8,48,64]{2,1,0:T(8,128)(2,1)} %get-tuple-element.111) | copy-start | bytes 147460
  133.0 1.5 copy-start.3
  139.7 1.7 copy-start.5
  143.2 8.8 %all-to-all-start.4 = ((bf16[8,12,512]{2,1,0:T(8,128)(2,1)}), bf16[8,12,512]{2,1,0:T(8,128)(2,1)S(1)}, u32[]{:S(2)}, u32[]{:S(2)}) async-start(bf16[8,12,512]{2,1,0:T(8,128)(2,1)} %all_to_all.65), calls=%async_computation.4 | async-start | bytes 262144 | tf_op jit(solution)/shard_map/all_to_all | solution.py:201
  152.0 10.3 %all-to-all-start.5 = ((bf16[8,12,512]{2,1,0:T(8,128)(2,1)}), bf16[8,12,512]{2,1,0:T(8,128)(2,1)S(1)}, u32[]{:S(2)}, u32[]{:S(2)}) async-start(bf16[8,12,512]{2,1,0:T(8,128)(2,1)} %all_to_all.68), calls=%async_computation.5 | async-start | bytes 262144 | tf_op jit(solution)/shard_map/all_to_all | solution.py:202
  162.2 9.4 %all-to-all-start.6 = ((bf16[8,12,512]{2,1,0:T(8,128)(2,1)}), bf16[8,12,512]{2,1,0:T(8,128)(2,1)S(1)}, u32[]{:S(2)}, u32[]{:S(2)}) async-start(bf16[8,12,512]{2,1,0:T(8,128)(2,1)} %all_to_all.71), calls=%async_computation.6 | async-start | bytes 262144 | tf_op jit(solution)/shard_map/all_to_all | solution.py:203
Sparse Core Ops, SparseCore 0:
  25.7 27.5 all-gather.4
  134.6 38.3 reduce-scatter.1
